TPU v7x, 256 devices: a whole 4x4x8 slice. The times are simulated.
256 devices in a mesh: dom: 32 (over y, z), feat: 8 (over x, core).
Axes of the slice: x: 4, y: 4, z: 8, core: 2. Of those that a mesh axis runs over, the one named last changes fastest.
Arguments:
- feats: bfloat16 [131072, 1024], P('dom', 'feat'), may hold values from -6 to 6
- projection: bfloat16 [1024, 512], P('feat'), may hold values from -0.1875 to 0.1875
- tiles: bfloat16 [8192, 4, 128, 128], P(('dom', 'feat')), may hold values from -0.25 to 0.25
- slot_owner: int32 [8192, 1], P(('dom', 'feat')), may hold values from 0 to 31; in each aligned block of 32 rows (0 to 31, 32 to 63, ...) at most 2 rows name the same one
- slot_block: int32 [8192, 1], P(('dom', 'feat')), may hold values from 0 to 3
- source_block: int32 [8192, 4], P(('dom', 'feat')), may hold values from 0 to 3
- counts: int32 [131072], P(('dom', 'feat')), may hold values from 1 to 4
- out_grad: bfloat16 [131072, 256], P(('dom', 'feat')), may hold values from -0.015625 to 0.015625
Outputs:
- activated: bfloat16 [131072, 256], P(('dom', 'feat'))
- weight_grad: float32 [1024, 512], P('feat')
Inputs may be any that keep to these rules, and one draw needn't show every extreme that they name: `slot_owner`: among the 32 sent rows of one device, no dom index is named more than 2 times; some device names one exactly 2 times.
All inputs are finite; a program needn't handle non-finite values.
Results may differ from a plain program's by a relative error of at most 0.0059.
Values may be sent and summed in bfloat16 or wider, within the bound.
A program may use at most 128 MiB of HBM per device.

v0:
```python
import jax
import jax.numpy as jnp
from jax import lax
from jax.sharding import PartitionSpec as P


def local(feats, projection, tiles, slot_owner, slot_block, source_block, counts, out_grad):
    tile_size = tiles.shape[-1]
    slot_count = tiles.shape[0]
    per_slot = tiles.shape[1]
    out_width = out_grad.shape[1]
    node_rows = out_grad.shape[0]
    block_count = node_rows // tile_size
    dom_count = lax.axis_size("dom")
    capacity = max(2, 2 * slot_count // dom_count)
    flat_width = tile_size * out_width
    projected = lax.psum_scatter(
        jnp.dot(feats, projection, preferred_element_type=jnp.float32),
        "feat",
        scatter_dimension=0,
        tiled=True,
    ).astype(jnp.bfloat16)
    neighbour = projected[:, :out_width].reshape(block_count, tile_size, out_width)
    self_part = projected[:, out_width:]
    picked = neighbour[source_block]
    contribution = jnp.einsum("skij,skjh->sih", tiles, picked, preferred_element_type=jnp.float32)
    contribution = contribution.astype(jnp.bfloat16).reshape(slot_count, flat_width)
    slot_dest = slot_owner[:, 0]
    dest_block = slot_block[:, 0]
    dest_hot = (slot_dest[:, None] == jnp.arange(dom_count, dtype=jnp.int32)[None, :]).astype(
        jnp.int32
    )
    before = jnp.cumsum(dest_hot, axis=0) - dest_hot
    position = jnp.sum(before * dest_hot, axis=1)
    slot_index = slot_dest * capacity + position
    placing = jnp.arange(dom_count * capacity, dtype=jnp.int32)[:, None] == slot_index[None, :]
    outgoing = jnp.dot(
        placing.astype(jnp.bfloat16), contribution, preferred_element_type=jnp.float32
    )
    outgoing = outgoing.astype(jnp.bfloat16).reshape(dom_count, capacity, flat_width)
    labels = jnp.sum(placing.astype(jnp.int32) * (dest_block + 1)[None, :], axis=1) - 1
    labels = labels.reshape(dom_count, capacity)
    incoming, got_labels = (
        lax.all_to_all(outgoing, "dom", split_axis=0, concat_axis=0, tiled=True),
        lax.all_to_all(labels, "dom", split_axis=0, concat_axis=0, tiled=True),
    )
    incoming = incoming.reshape(dom_count * capacity, flat_width)
    receive_hot = (
        jnp.arange(block_count, dtype=jnp.int32)[:, None] == got_labels.reshape(-1)[None, :]
    ).astype(jnp.bfloat16)
    summed = jnp.dot(receive_hot, incoming, preferred_element_type=jnp.float32).reshape(
        node_rows, out_width
    )
    degree = counts.astype(jnp.float32)[:, None]
    preact = summed / degree + self_part.astype(jnp.float32)
    sigma = jax.nn.sigmoid(preact)
    activated = (preact * sigma).astype(jnp.bfloat16)
    grad_pre = out_grad.astype(jnp.float32) * sigma * (1.0 + preact * (1.0 - sigma))
    grad_self = grad_pre.astype(jnp.bfloat16)
    grad_sum = (grad_pre / degree).astype(jnp.bfloat16).reshape(block_count, flat_width)
    sending_back = jnp.dot(receive_hot.T, grad_sum, preferred_element_type=jnp.float32)
    sending_back = sending_back.astype(jnp.bfloat16).reshape(dom_count, capacity, flat_width)
    returned = lax.all_to_all(sending_back, "dom", split_axis=0, concat_axis=0, tiled=True).reshape(
        dom_count * capacity, flat_width
    )
    slot_grad = jnp.dot(
        placing.T.astype(jnp.bfloat16), returned, preferred_element_type=jnp.float32
    )
    slot_grad = slot_grad.astype(jnp.bfloat16).reshape(slot_count, tile_size, out_width)
    products = jnp.einsum("skij,sih->skjh", tiles, slot_grad, preferred_element_type=jnp.float32)
    source_hot = (
        jnp.arange(block_count, dtype=jnp.int32)[:, None] == source_block.reshape(-1)[None, :]
    ).astype(jnp.float32)
    flat_products = products.reshape(slot_count * per_slot, tile_size, out_width)
    grad_neigh = jnp.einsum(
        "bn,njh->bjh", source_hot, flat_products, precision=lax.Precision.HIGHEST
    )
    grad_neigh = grad_neigh.astype(jnp.bfloat16).reshape(node_rows, out_width)
    grad_proj = jnp.concatenate([grad_neigh, grad_self], axis=1)
    partial_grad = lax.dot_general(
        feats,
        lax.all_gather(grad_proj, "feat", axis=0, tiled=True),
        (((0,), (0,)), ((), ())),
        preferred_element_type=jnp.float32,
    )
    weight_grad = lax.psum(partial_grad, "dom")
    return (activated, weight_grad)


def solution(mesh):
    placed = (
        P("dom", "feat"),
        P("feat", None),
        P(("dom", "feat"), None, None, None),
        P(("dom", "feat"), None),
        P(("dom", "feat"), None),
        P(("dom", "feat"), None),
        P(("dom", "feat")),
        P(("dom", "feat"), None),
    )
    return jax.shard_map(
        local,
        mesh=mesh,
        in_specs=placed,
        out_specs=(P(("dom", "feat"), None), P("feat", None)),
        check_vma=False,
    )
```

profile of v0, /device:TPU:2, one launch (start us, length us, event | category | flops | bytes accessed | tf_op | source)
XLA Modules:
  0.0 570.8 jit_solution(17779581834681642743)
XLA Ops:
  7.2 0.0 copy-start
  7.2 0.0 reduce-scatter.2.cloned.1.call-start
  7.2 1.2 copy-done
  8.4 5.4 fusion.12
  13.8 0.0 copy-start.6
  13.8 0.0 copy-start.8
  13.8 0.0 copy-start.5
  13.8 0.0 reduce-scatter.2.cloned.1.call-update
  13.8 0.6 copy-done.6
  14.4 0.1 fusion.3
  14.5 0.1 reduce_window_sum.11
  14.6 0.2 select_reduce_fusion.1
  14.7 0.0 copy-done.8
  14.8 0.1 select_reduce_fusion
  14.9 0.7 sub.14
  15.6 11.5 %all-to-all-start = ((s32[32,1,2]{2,1,0:T(1,128)}), s32[32,1,2]{2,1,0:T(1,128)S(1)}, u32[]{:S(2)}, u32[]{:S(2)}) async-start(s32[32,1,2]{2,1,0:T(1,128)} %bitcast.2), calls=%async_computation | async-start | bytes 32768 | tf_op jit(solution)/shard_map/all_to_all | solution.py:45
  27.1 0.0 copy-done.5
  27.1 0.1 copy.35
  27.2 0.1 reshape.85
  27.3 42.2 %reduce-scatter.2.cloned.1.call-done = f32[512,512]{1,0:T(8,128)} async-done(((f32[4096,512]{1,0:T(8,128)}), f32[512,512]{1,0:T(8,128)}) %reduce-scatter.2.cloned.1.call-update) | async-done | bytes 1048592 | tf_op jit(solution)/shard_map/reduce_scatter | solution.py:17
  69.5 1.3 convert_element_type.48
  70.8 0.0 copy-start.2
  70.8 0.8 copy-done.2
  71.7 6.5 %gather_fusion = bf16[128,128,256]{2,1,0:T(8,128)(2,1)} fusion(bf16[4,128,256]{2,1,0:T(8,128)(2,1)S(1)} %bitcast.46, s32[1024]{0:T(1024)S(1)} %pad_clamp_fusion), kind=kCustom, calls=%fused_computation | custom fusion | bytes 16777728 | tf_op jit(solution)/shard_map/gather | solution.py:25
  78.2 7.0 %fusion.2 = bf16[32,128,256]{1,2,0:T(8,128)(2,1)S(1)} fusion(bf16[32,4,128,256]{3,2,1,0:T(8,128)(2,1)} %bitcast.48, bf16[32,4,128,128]{3,2,1,0:T(8,128)(2,1)} %param.10), kind=kOutput, calls=%fused_computation.7 | convolution fusion | flops 1074790400 | bytes 14680064 | tf_op jit(solution)/shard_map/skij,skjh->sih/dot_general | solution.py:26
  85.2 2.9 copy.47
  88.1 4.9 convolution_convert_fusion.1
  93.0 7.6 %reshape.74 = bf16[32,2,32768]{2,1,0:T(2,128)(2,1)} reshape(bf16[64,32768]{1,0:T(8,128)(2,1)} %convolution_convert_fusion.1) | data formatting | bytes 8388608 | tf_op jit(solution)/shard_map/reshape | solution.py:40
  100.6 0.0 all-to-all-done
  100.6 10.5 %all-to-all-start.1 = ((bf16[32,2,32768]{2,1,0:T(2,128)(2,1)}), bf16[32,2,32768]{2,1,0:T(2,128)(2,1)}, u32[]{:S(2)}, u32[]{:S(2)}) async-start(bf16[32,2,32768]{2,1,0:T(2,128)(2,1)} %reshape.74), calls=%async_computation.2 | async-start | bytes 8388608 | tf_op jit(solution)/shard_map/all_to_all | solution.py:44
  111.2 0.0 copy-done.7
  111.2 0.5 broadcast.49
  111.7 0.7 reduce.3
  112.4 0.1 eq.63
  112.5 96.4 %all-to-all-done.1 = bf16[32,2,32768]{2,1,0:T(2,128)(2,1)} async-done(((bf16[32,2,32768]{2,1,0:T(2,128)(2,1)}), bf16[32,2,32768]{2,1,0:T(2,128)(2,1)}, u32[]{:S(2)}, u32[]{:S(2)}) %all-to-all-start.1) | async-done | bytes 4194336 | tf_op jit(solution)/shard_map/all_to_all | solution.py:44
  208.9 7.3 %reshape.75 = bf16[64,32768]{1,0:T(8,128)(2,1)} reshape(bf16[32,2,32768]{2,1,0:T(2,128)(2,1)} %all-to-all-done.1) | data formatting | bytes 8388608 | tf_op jit(solution)/shard_map/reshape | solution.py:47
  216.2 2.9 fusion.6
  219.1 0.4 reshape.76
  219.5 0.0 copy-done.3
  219.5 0.0 copy-done.4
  219.5 1.1 divide_convert_fusion
  220.6 0.2 reshape.77
  220.8 3.2 convolution_convert_fusion
  224.0 7.6 %reshape.78 = bf16[32,2,32768]{2,1,0:T(2,128)(2,1)} reshape(bf16[64,32768]{1,0:T(8,128)(2,1)} %convolution_convert_fusion) | data formatting | bytes 8388608 | tf_op jit(solution)/shard_map/reshape | solution.py:62
  231.7 8.5 %all-to-all-start.2 = ((bf16[32,2,32768]{2,1,0:T(2,128)(2,1)}), bf16[32,2,32768]{2,1,0:T(2,128)(2,1)}, u32[]{:S(2)}, u32[]{:S(2)}) async-start(bf16[32,2,32768]{2,1,0:T(2,128)(2,1)} %reshape.78), calls=%async_computation.3 | async-start | bytes 8388608 | tf_op jit(solution)/shard_map/all_to_all | solution.py:63
  240.2 0.0 all-gather.2.cloned.1.call-start
  240.2 0.1 copy.38
  240.3 0.1 eq.67
  240.4 95.7 %all-to-all-done.2 = bf16[32,2,32768]{2,1,0:T(2,128)(2,1)} async-done(((bf16[32,2,32768]{2,1,0:T(2,128)(2,1)}), bf16[32,2,32768]{2,1,0:T(2,128)(2,1)}, u32[]{:S(2)}, u32[]{:S(2)}) %all-to-all-start.2) | async-done | bytes 4194336 | tf_op jit(solution)/shard_map/all_to_all | solution.py:63
  336.1 7.3 %reshape.79 = bf16[64,32768]{1,0:T(8,128)(2,1)} reshape(bf16[32,2,32768]{2,1,0:T(2,128)(2,1)} %all-to-all-done.2) | data formatting | bytes 8388608 | tf_op jit(solution)/shard_map/reshape | solution.py:63
  343.4 3.1 convolution_convert_fusion.2
  346.5 0.5 copy.48
  347.0 0.0 copy-done.1
  347.0 8.1 %fusion = f32[32,256,4,128]{3,1,2,0:T(8,128)} fusion(bf16[32,4,128,128]{3,2,1,0:T(8,128)(2,1)S(1)} %copy-done.1, bf16[32,128,256]{2,1,0:T(8,128)(2,1)S(1)} %bitcast.52), kind=kOutput, calls=%fused_computation.5 | convolution fusion | flops 1073741824 | bytes 23068672 | tf_op jit(solution)/shard_map/skij,sih->skjh/dot_general | solution.py:70
  355.1 17.7 %copy.40 = f32[128,128,256]{2,0,1:T(8,128)} copy(f32[128,128,256]{1,2,0:T(8,128)} %bitcast.47) | data formatting | bytes 33554432 | tf_op jit(solution)/shard_map/reshape | solution.py:74
  372.8 9.0 %convolution_convert_fusion.3 = bf16[4,128,256]{2,0,1:T(4,128)(2,1)S(1)} fusion(f32[128,128,256]{2,0,1:T(8,128)} %copy.40, s32[128]{0:T(128)S(1)} %eq.67), kind=kOutput, calls=%fused_computation.8 | convolution fusion | flops 201458176 | bytes 17039872 | tf_op jit(solution)/shard_map/bn,njh->bjh/dot_general | solution.py:75
  381.8 0.8 pad_maximum_fusion
  382.7 0.0 all-gather.2.cloned.1.call-update
  382.7 0.0 all-reduce.2.cloned.1.call-start
  382.7 30.2 %all-gather.2.cloned.1.call-done = bf16[4096,512]{1,0:T(8,128)(2,1)} async-done(((bf16[512,512]{1,0:T(8,128)(2,1)}), bf16[4096,512]{1,0:T(8,128)(2,1)}) %all-gather.2.cloned.1.call-update) | async-done | bytes 4194320 | tf_op jit(solution)/shard_map/all_gather | solution.py:82
  413.0 4.2 convolution_bitcast_fusion
  417.2 0.0 all-reduce.2.cloned.1.call-update
  417.2 145.3 %all-reduce.2.cloned.1.call-done = f32[128,512]{0,1:T(8,128)} async-done(((f32[128,512]{0,1:T(8,128)}), f32[128,512]{0,1:T(8,128)}) %all-reduce.2.cloned.1.call-update) | async-done | bytes 262160 | tf_op jit(solution)/shard_map/psum | solution.py:86
  562.5 1.8 copy.42
  (12 shorter events, 0.1 us)
Async XLA Ops:
  7.2 1.2 copy-start
  7.2 62.4 %reduce-scatter.2.cloned.1.call-start = ((), (), s32[]{:S(2)}) async-start(), calls=%async_computation.4 | async-start | bytes 9437184 | tf_op jit(solution)/shard_map/reduce_scatter | solution.py:17
  13.8 0.7 copy-start.6
  13.8 1.0 copy-start.8
  13.8 13.3 %copy-start.5 = (s32[32,4]{0,1:T(4,128)S(1)}, s32[32,4]{0,1:T(4,128)}, u32[]{:S(2)}) copy-start(s32[32,4]{0,1:T(4,128)} %param.13) | copy-start | bytes 1540
  15.6 85.1 %all-to-all-start = ((s32[32,1,2]{2,1,0:T(1,128)}), s32[32,1,2]{2,1,0:T(1,128)S(1)}, u32[]{:S(2)}, u32[]{:S(2)}) async-start(s32[32,1,2]{2,1,0:T(1,128)} %bitcast.2), calls=%async_computation | async-start | bytes 32768 | tf_op jit(solution)/shard_map/all_to_all | solution.py:45
  70.8 0.8 copy-start.2
  100.6 10.5 %copy-start.7 = (s32[512]{0:T(512)S(1)}, s32[512]{0:T(512)}, u32[]{:S(2)}) copy-start(s32[512]{0:T(512)} %param.14) | copy-start | bytes 6148
  100.6 108.3 %all-to-all-start.1 = ((bf16[32,2,32768]{2,1,0:T(2,128)(2,1)}), bf16[32,2,32768]{2,1,0:T(2,128)(2,1)}, u32[]{:S(2)}, u32[]{:S(2)}) async-start(bf16[32,2,32768]{2,1,0:T(2,128)(2,1)} %reshape.74), calls=%async_computation.2 | async-start | bytes 8388608 | tf_op jit(solution)/shard_map/all_to_all | solution.py:44
  216.2 3.3 copy-start.3
  216.2 3.3 copy-start.4
  231.7 104.5 %all-to-all-start.2 = ((bf16[32,2,32768]{2,1,0:T(2,128)(2,1)}), bf16[32,2,32768]{2,1,0:T(2,128)(2,1)}, u32[]{:S(2)}, u32[]{:S(2)}) async-start(bf16[32,2,32768]{2,1,0:T(2,128)(2,1)} %reshape.78), calls=%async_computation.3 | async-start | bytes 8388608 | tf_op jit(solution)/shard_map/all_to_all | solution.py:63
  240.2 172.8 %all-gather.2.cloned.1.call-start = ((), (), s32[]{:S(2)}) async-start(), calls=%async_computation.5 | async-start | bytes 4718592 | tf_op jit(solution)/shard_map/all_gather | solution.py:82
  343.4 3.6 copy-start.1
  382.7 179.8 %all-reduce.2.cloned.1.call-start = ((), (), s32[]{:S(2)}) async-start(), calls=%async_computation.6 | async-start | bytes 524288 | tf_op jit(solution)/shard_map/psum | solution.py:86
Sparse Core Ops, SparseCore 0:
  13.9 55.5 reduce-scatter.1
  382.8 30.1 all-gather.1
  417.3 145.1 all-reduce.1
where the time goes:
time: 572 us; the launch traced here: 571 us
  waiting for transfers between devices  410 us (72%)
  local copies, waits for them, and re-layouts  64.1 us (11%)
  matrix products  47.8 us (8%)
  starting transfers between devices  30.6 us (5%)
  between operations  13.9 us (2%)
    psum x1, waiting for transfers between devices, local(): weight_grad = lax.psum(partial_grad, 'dom')  145 us
    all_to_all x1, waiting for transfers between devices, local(): lax.all_to_all(outgoing, 'dom', split_axis=0, concat_axis=0, tiled=True)  96.4 us
    all_to_all x1, waiting for transfers between devices, local(): lax.all_to_all(sending_back, 'dom', split_axis=0, concat_axis=0, tiled=True)  95.7 us
    reduce_scatter x1, waiting for transfers between devices, local(): lax.psum_scatter(jnp.dot(feats, projection, preferred_element_type=jnp.fl...  42.2 us
    all_gather x1, waiting for transfers between devices, local(): lax.all_gather(grad_proj, 'feat', axis=0, tiled=True)  30.2 us
    reshape x1, local copies, waits for them, and re-layouts, local(): products.reshape(slot_count * per_slot, tile_size, out_width)  17.7 us
    all_to_all x1, starting transfers between devices, local(): lax.all_to_all(labels, 'dom', split_axis=0, concat_axis=0, tiled=True)  11.5 us
  transfers between devices with their start and end apart: 6, of which 5 were waited for; matrix products, arithmetic and copies ran while one was open for 6% of the time, Pallas kernels for 0%

commit v1 on v0

--- a/solution.py
+++ b/solution.py
@@ -83,7 +83,12 @@
         (((0,), (0,)), ((), ())),
         preferred_element_type=jnp.float32,
     )
-    weight_grad = lax.psum(partial_grad, "dom")
+    num_devices = lax.axis_size("dom")
+    weight_grad = partial_grad
+    for b in [
+        [(c, c ^ pp) for c in range(num_devices)] for pp in (1, 2, 4, 8, 16) if pp < num_devices
+    ]:
+        weight_grad = weight_grad + lax.ppermute(weight_grad, "dom", b)
     return (activated, weight_grad)
 
 

time: 572 us -> 484 us (0.85)
  waiting for transfers between devices: 410 us -> 305 us
  starting transfers between devices: 30.6 us -> 46.4 us
    psum x1 -> x0, waiting for transfers between devices: 145 us -> none  [local(): weight_grad = lax.psum(partial_grad, 'dom')]
    ppermute x0 -> x5, waiting for transfers between devices: none -> 40.2 us  [local(): weight_grad = weight_grad + lax.ppermute(weight_grad, 'dom', b)]
    ppermute x0 -> x5, starting transfers between devices: none -> 15.8 us  [local(): weight_grad = weight_grad + lax.ppermute(weight_grad, 'dom', b)]
  transfers between devices with their start and end apart: 6 -> 10, of which waited for: 5 -> 9; matrix products, arithmetic and copies ran while one was open for 6% -> 7% of each run, Pallas kernels for 0% -> 0%
where the time goes in v1:
time: 484 us; the launch traced here: 480 us
  waiting for transfers between devices  305 us (63%)
  local copies, waits for them, and re-layouts  63.3 us (13%)
  matrix products  47.1 us (10%)
  starting transfers between devices  46.4 us (10%)
  between operations  14.3 us (3%)
    all_to_all x1, waiting for transfers between devices, local(): lax.all_to_all(outgoing, 'dom', split_axis=0, concat_axis=0, tiled=True)  96.4 us
    all_to_all x1, waiting for transfers between devices, local(): lax.all_to_all(sending_back, 'dom', split_axis=0, concat_axis=0, tiled=True)  95.7 us
    reduce_scatter x1, waiting for transfers between devices, local(): lax.psum_scatter(jnp.dot(feats, projection, preferred_element_type=jnp.fl...  42.2 us
    ppermute x5, waiting for transfers between devices, local(): weight_grad = weight_grad + lax.ppermute(weight_grad, 'dom', b)  40.2 us
    all_gather x1, waiting for transfers between devices, local(): lax.all_gather(grad_proj, 'feat', axis=0, tiled=True)  30.3 us
    reshape x1, local copies, waits for them, and re-layouts, local(): products.reshape(slot_count * per_slot, tile_size, out_width)  17.7 us
    ppermute x5, starting transfers between devices, local(): weight_grad = weight_grad + lax.ppermute(weight_grad, 'dom', b)  15.8 us
    all_to_all x1, starting transfers between devices, local(): lax.all_to_all(labels, 'dom', split_axis=0, concat_axis=0, tiled=True)  11.5 us
  transfers between devices with their start and end apart: 10, of which 9 were waited for; matrix products, arithmetic and copies ran while one was open for 7% of the time, Pallas kernels for 0%

profile of v1, /device:TPU:2, one launch (start us, length us, event | category | flops | bytes accessed | tf_op | source)
XLA Modules:
  0.0 480.4 jit_solution(16887241822676697801)
XLA Ops:
  7.2 0.0 copy-start
  7.2 0.0 reduce-scatter.2.cloned.1.call-start
  7.2 1.2 copy-done
  8.4 5.3 %fusion.12 = f32[4096,512]{1,0:T(8,128)} fusion(bf16[4096,128]{1,0:T(8,128)(2,1)S(1)} %copy-done, bf16[128,512]{1,0:T(8,128)(2,1)} %param.9), kind=kOutput, calls=%fused_computation.35 | convolution fusion | flops 536870912 | bytes 9568256 | tf_op jit(solution)/shard_map/dot_general | solution.py:18
  13.7 0.0 reduce-scatter.2.cloned.1.call-update
  13.8 0.6 copy-done.6
  14.4 0.1 fusion.3
  14.5 0.1 reduce_window_sum.11
  14.5 0.2 select_reduce_fusion.1
  14.7 0.0 copy-done.8
  14.7 0.1 select_reduce_fusion
  14.8 0.7 sub.14
  15.6 11.5 %all-to-all-start = ((s32[32,1,2]{2,1,0:T(1,128)}), s32[32,1,2]{2,1,0:T(1,128)S(1)}, u32[]{:S(2)}, u32[]{:S(2)}) async-start(s32[32,1,2]{2,1,0:T(1,128)} %bitcast.2), calls=%async_computation | async-start | bytes 32768 | tf_op jit(solution)/shard_map/all_to_all | solution.py:45
  27.0 0.0 copy-done.5
  27.1 0.1 copy.35
  27.2 0.1 reshape.85
  27.3 42.2 %reduce-scatter.2.cloned.1.call-done = f32[512,512]{1,0:T(8,128)} async-done(((f32[4096,512]{1,0:T(8,128)}), f32[512,512]{1,0:T(8,128)}) %reduce-scatter.2.cloned.1.call-update) | async-done | bytes 1048592 | tf_op jit(solution)/shard_map/reduce_scatter | solution.py:17
  69.5 1.3 convert_element_type.48
  70.8 0.0 copy-start.2
  70.8 0.8 copy-done.2
  71.7 6.5 %gather_fusion = bf16[128,128,256]{2,1,0:T(8,128)(2,1)} fusion(bf16[4,128,256]{2,1,0:T(8,128)(2,1)S(1)} %bitcast.46, s32[1024]{0:T(1024)S(1)} %pad_clamp_fusion), kind=kCustom, calls=%fused_computation | custom fusion | bytes 16777728 | tf_op jit(solution)/shard_map/gather | solution.py:25
  78.1 7.0 %fusion.2 = bf16[32,128,256]{1,2,0:T(8,128)(2,1)S(1)} fusion(bf16[32,4,128,256]{3,2,1,0:T(8,128)(2,1)} %bitcast.48, bf16[32,4,128,128]{3,2,1,0:T(8,128)(2,1)} %param.10), kind=kOutput, calls=%fused_computation.7 | convolution fusion | flops 1074790400 | bytes 14680064 | tf_op jit(solution)/shard_map/skij,skjh->sih/dot_general | solution.py:26
  85.1 2.9 copy.47
  88.0 4.9 %convolution_convert_fusion.1 = bf16[64,32768]{1,0:T(8,128)(2,1)} fusion(bf16[32,32768]{1,0:T(8,128)(2,1)} %bitcast.51, s32[32]{0:T(128)S(1)} %multiply_add_fusion), kind=kOutput, calls=%fused_computation.2 | convolution fusion | flops 136316928 | bytes 6291584 | tf_op jit(solution)/shard_map/dot_general | solution.py:37
  92.9 7.7 %reshape.74 = bf16[32,2,32768]{2,1,0:T(2,128)(2,1)} reshape(bf16[64,32768]{1,0:T(8,128)(2,1)} %convolution_convert_fusion.1) | data formatting | bytes 8388608 | tf_op jit(solution)/shard_map/reshape | solution.py:40
  100.6 0.0 all-to-all-done
  100.6 10.5 %all-to-all-start.1 = ((bf16[32,2,32768]{2,1,0:T(2,128)(2,1)}), bf16[32,2,32768]{2,1,0:T(2,128)(2,1)}, u32[]{:S(2)}, u32[]{:S(2)}) async-start(bf16[32,2,32768]{2,1,0:T(2,128)(2,1)} %reshape.74), calls=%async_computation.2 | async-start | bytes 8388608 | tf_op jit(solution)/shard_map/all_to_all | solution.py:44
  111.2 0.5 broadcast.49
  111.7 0.7 reduce.3
  112.4 0.1 eq.63
  112.5 96.4 %all-to-all-done.1 = bf16[32,2,32768]{2,1,0:T(2,128)(2,1)} async-done(((bf16[32,2,32768]{2,1,0:T(2,128)(2,1)}), bf16[32,2,32768]{2,1,0:T(2,128)(2,1)}, u32[]{:S(2)}, u32[]{:S(2)}) %all-to-all-start.1) | async-done | bytes 4194336 | tf_op jit(solution)/shard_map/all_to_all | solution.py:44
  208.9 7.3 %reshape.75 = bf16[64,32768]{1,0:T(8,128)(2,1)} reshape(bf16[32,2,32768]{2,1,0:T(2,128)(2,1)} %all-to-all-done.1) | data formatting | bytes 8388608 | tf_op jit(solution)/shard_map/reshape | solution.py:47
  216.2 2.9 fusion.6
  219.1 0.4 reshape.76
  219.5 1.1 divide_convert_fusion
  220.6 0.2 reshape.77
  220.8 3.3 convolution_convert_fusion
  224.0 7.7 %reshape.78 = bf16[32,2,32768]{2,1,0:T(2,128)(2,1)} reshape(bf16[64,32768]{1,0:T(8,128)(2,1)} %convolution_convert_fusion) | data formatting | bytes 8388608 | tf_op jit(solution)/shard_map/reshape | solution.py:62
  231.7 8.5 %all-to-all-start.2 = ((bf16[32,2,32768]{2,1,0:T(2,128)(2,1)}), bf16[32,2,32768]{2,1,0:T(2,128)(2,1)}, u32[]{:S(2)}, u32[]{:S(2)}) async-start(bf16[32,2,32768]{2,1,0:T(2,128)(2,1)} %reshape.78), calls=%async_computation.3 | async-start | bytes 8388608 | tf_op jit(solution)/shard_map/all_to_all | solution.py:63
  240.2 0.0 all-gather.2.cloned.1.call-start
  240.3 0.1 copy.38
  240.4 0.1 eq.67
  240.5 95.7 %all-to-all-done.2 = bf16[32,2,32768]{2,1,0:T(2,128)(2,1)} async-done(((bf16[32,2,32768]{2,1,0:T(2,128)(2,1)}), bf16[32,2,32768]{2,1,0:T(2,128)(2,1)}, u32[]{:S(2)}, u32[]{:S(2)}) %all-to-all-start.2) | async-done | bytes 4194336 | tf_op jit(solution)/shard_map/all_to_all | solution.py:63
  336.2 7.3 %reshape.79 = bf16[64,32768]{1,0:T(8,128)(2,1)} reshape(bf16[32,2,32768]{2,1,0:T(2,128)(2,1)} %all-to-all-done.2) | data formatting | bytes 8388608 | tf_op jit(solution)/shard_map/reshape | solution.py:63
  343.5 3.1 convolution_convert_fusion.2
  346.6 0.5 copy.48
  347.1 8.1 %fusion = f32[32,256,4,128]{3,1,2,0:T(8,128)} fusion(bf16[32,4,128,128]{3,2,1,0:T(8,128)(2,1)S(1)} %copy-done.1, bf16[32,128,256]{2,1,0:T(8,128)(2,1)S(1)} %bitcast.52), kind=kOutput, calls=%fused_computation.5 | convolution fusion | flops 1073741824 | bytes 23068672 | tf_op jit(solution)/shard_map/skij,sih->skjh/dot_general | solution.py:70
  355.2 17.7 %copy.40 = f32[128,128,256]{2,0,1:T(8,128)} copy(f32[128,128,256]{1,2,0:T(8,128)} %bitcast.47) | data formatting | bytes 33554432 | tf_op jit(solution)/shard_map/reshape | solution.py:74
  372.9 9.0 %convolution_convert_fusion.3 = bf16[4,128,256]{2,0,1:T(4,128)(2,1)S(1)} fusion(f32[128,128,256]{2,0,1:T(8,128)} %copy.40, s32[128]{0:T(128)S(1)} %eq.67), kind=kOutput, calls=%fused_computation.8 | convolution fusion | flops 201458176 | bytes 17039872 | tf_op jit(solution)/shard_map/bn,njh->bjh/dot_general | solution.py:75
  381.9 0.8 pad_maximum_fusion
  382.8 0.0 all-gather.2.cloned.1.call-update
  382.8 30.3 %all-gather.2.cloned.1.call-done = bf16[4096,512]{1,0:T(8,128)(2,1)} async-done(((bf16[512,512]{1,0:T(8,128)(2,1)}), bf16[4096,512]{1,0:T(8,128)(2,1)}) %all-gather.2.cloned.1.call-update) | async-done | bytes 4194320 | tf_op jit(solution)/shard_map/all_gather | solution.py:82
  413.1 3.5 convolution_bitcast_fusion
  416.6 1.6 collective-permute-start
  418.2 6.9 %collective-permute-done = f32[128,512]{0,1:T(8,128)S(1)} collective-permute-done((f32[128,512]{0,1:T(8,128)S(1)}, f32[128,512]{0,1:T(8,128)S(1)}, u32[]{:S(2)}, u32[]{:S(2)}) %collective-permute-start) | collective-permute-done | bytes 262176 | tf_op jit(solution)/shard_map/ppermute | solution.py:91
  425.1 2.6 collective-permute-start.1
  427.8 11.6 %collective-permute-done.1 = f32[128,512]{0,1:T(8,128)S(1)} collective-permute-done((f32[128,512]{0,1:T(8,128)S(1)}, f32[128,512]{0,1:T(8,128)S(1)}, u32[]{:S(2)}, u32[]{:S(2)}) %collective-permute-start.1) | collective-permute-done | bytes 262176 | tf_op jit(solution)/shard_map/ppermute | solution.py:91
  439.4 5.8 %collective-permute-start.2 = (f32[128,512]{0,1:T(8,128)S(1)}, f32[128,512]{0,1:T(8,128)S(1)}, u32[]{:S(2)}, u32[]{:S(2)}) collective-permute-start(f32[128,512]{0,1:T(8,128)S(1)} %add.72), channel_id=1, source_target_pairs={{0,32},{8,40},{16,48},{24,56},{32,0},{40,8},{48,16},{56,24},{64,96... | collective-permute-start | bytes 786440 | tf_op jit(solution)/shard_map/ppermute | solution.py:91
  445.2 12.1 %collective-permute-done.2 = f32[128,512]{0,1:T(8,128)S(1)} collective-permute-done((f32[128,512]{0,1:T(8,128)S(1)}, f32[128,512]{0,1:T(8,128)S(1)}, u32[]{:S(2)}, u32[]{:S(2)}) %collective-permute-start.2) | collective-permute-done | bytes 262176 | tf_op jit(solution)/shard_map/ppermute | solution.py:91
  457.3 1.6 collective-permute-start.3
  458.9 5.2 %collective-permute-done.3 = f32[128,512]{0,1:T(8,128)S(1)} collective-permute-done((f32[128,512]{0,1:T(8,128)S(1)}, f32[128,512]{0,1:T(8,128)S(1)}, u32[]{:S(2)}, u32[]{:S(2)}) %collective-permute-start.3) | collective-permute-done | bytes 262176 | tf_op jit(solution)/shard_map/ppermute | solution.py:91
  464.2 4.1 collective-permute-start.4
  468.3 4.4 collective-permute-done.4
  472.7 0.8 copy.42
  (24 shorter events, 0.2 us)
Async XLA Ops:
  7.2 1.2 copy-start
  7.2 62.3 %reduce-scatter.2.cloned.1.call-start = ((), (), s32[]{:S(2)}) async-start(), calls=%async_computation.4 | async-start | bytes 9437184 | tf_op jit(solution)/shard_map/reduce_scatter | solution.py:17
  13.7 0.7 copy-start.6
  13.7 1.0 copy-start.8
  13.7 13.3 %copy-start.5 = (s32[32,4]{0,1:T(4,128)S(1)}, s32[32,4]{0,1:T(4,128)}, u32[]{:S(2)}) copy-start(s32[32,4]{0,1:T(4,128)} %param.13) | copy-start | bytes 1540
  15.6 85.1 %all-to-all-start = ((s32[32,1,2]{2,1,0:T(1,128)}), s32[32,1,2]{2,1,0:T(1,128)S(1)}, u32[]{:S(2)}, u32[]{:S(2)}) async-start(s32[32,1,2]{2,1,0:T(1,128)} %bitcast.2), calls=%async_computation | async-start | bytes 32768 | tf_op jit(solution)/shard_map/all_to_all | solution.py:45
  70.8 0.8 copy-start.2
  100.6 10.5 %copy-start.7 = (s32[512]{0:T(512)S(1)}, s32[512]{0:T(512)}, u32[]{:S(2)}) copy-start(s32[512]{0:T(512)} %param.14) | copy-start | bytes 6148
  100.6 108.3 %all-to-all-start.1 = ((bf16[32,2,32768]{2,1,0:T(2,128)(2,1)}), bf16[32,2,32768]{2,1,0:T(2,128)(2,1)}, u32[]{:S(2)}, u32[]{:S(2)}) async-start(bf16[32,2,32768]{2,1,0:T(2,128)(2,1)} %reshape.74), calls=%async_computation.2 | async-start | bytes 8388608 | tf_op jit(solution)/shard_map/all_to_all | solution.py:44
  216.2 3.3 copy-start.3
  216.2 3.3 copy-start.4
  231.7 104.5 %all-to-all-start.2 = ((bf16[32,2,32768]{2,1,0:T(2,128)(2,1)}), bf16[32,2,32768]{2,1,0:T(2,128)(2,1)}, u32[]{:S(2)}, u32[]{:S(2)}) async-start(bf16[32,2,32768]{2,1,0:T(2,128)(2,1)} %reshape.78), calls=%async_computation.3 | async-start | bytes 8388608 | tf_op jit(solution)/shard_map/all_to_all | solution.py:63
  240.2 172.9 %all-gather.2.cloned.1.call-start = ((), (), s32[]{:S(2)}) async-start(), calls=%async_computation.5 | async-start | bytes 4718592 | tf_op jit(solution)/shard_map/all_gather | solution.py:82
  343.5 3.6 copy-start.1
  416.6 8.5 %collective-permute-start = (f32[128,512]{0,1:T(8,128)S(1)}, f32[128,512]{0,1:T(8,128)S(1)}, u32[]{:S(2)}, u32[]{:S(2)}) collective-permute-start(f32[128,512]{0,1:T(8,128)S(1)} %convolution_bitcast_fusion), channel_id=1, source_target_pairs={{0,8},{8,0},{16,24},{24,16},{32,40},{40,32},{48,56},{56,48},{64,72... | collective-permute-start | bytes 786440 | tf_op jit(solution)/shard_map/ppermute | solution.py:91
  425.1 14.2 %collective-permute-start.1 = (f32[128,512]{0,1:T(8,128)S(1)}, f32[128,512]{0,1:T(8,128)S(1)}, u32[]{:S(2)}, u32[]{:S(2)}) collective-permute-start(f32[128,512]{0,1:T(8,128)S(1)} %add.71), channel_id=1, source_target_pairs={{0,16},{8,24},{16,0},{24,8},{32,48},{40,56},{48,32},{56,40},{64,80... | collective-permute-start | bytes 786440 | tf_op jit(solution)/shard_map/ppermute | solution.py:91
  439.4 17.9 %collective-permute-start.2 = (f32[128,512]{0,1:T(8,128)S(1)}, f32[128,512]{0,1:T(8,128)S(1)}, u32[]{:S(2)}, u32[]{:S(2)}) collective-permute-start(f32[128,512]{0,1:T(8,128)S(1)} %add.72), channel_id=1, source_target_pairs={{0,32},{8,40},{16,48},{24,56},{32,0},{40,8},{48,16},{56,24},{64,96... | collective-permute-start | bytes 786440 | tf_op jit(solution)/shard_map/ppermute | solution.py:91
  457.3 6.8 %collective-permute-start.3 = (f32[128,512]{0,1:T(8,128)S(1)}, f32[128,512]{0,1:T(8,128)S(1)}, u32[]{:S(2)}, u32[]{:S(2)}) collective-permute-start(f32[128,512]{0,1:T(8,128)S(1)} %add.73), channel_id=1, source_target_pairs={{0,64},{8,72},{16,80},{24,88},{32,96},{40,104},{48,112},{56,120},{... | collective-permute-start | bytes 786440 | tf_op jit(solution)/shard_map/ppermute | solution.py:91
  464.2 8.5 %collective-permute-start.4 = (f32[128,512]{0,1:T(8,128)S(1)}, f32[128,512]{0,1:T(8,128)S(1)}, u32[]{:S(2)}, u32[]{:S(2)}) collective-permute-start(f32[128,512]{0,1:T(8,128)S(1)} %add.74), channel_id=1, source_target_pairs={{0,128},{8,136},{16,144},{24,152},{32,160},{40,168},{48,176},{56,1... | collective-permute-start | bytes 786440 | tf_op jit(solution)/shard_map/ppermute | solution.py:91
Sparse Core Ops, SparseCore 0:
  13.9 55.5 reduce-scatter.1
  382.9 30.1 all-gather.1
